TPU v7x, 32 devices: a whole 2x2x4 slice. The times are simulated.
32 devices in a mesh: fsdp: 8 (over z, x), tp: 4 (over y, core).
Axes of the slice: x: 2, y: 2, z: 4, core: 2. Of those that a mesh axis runs over, the one named last changes fastest.
Arguments:
- inputs: bfloat16 [2, 8, 1024, 2048], P(None, 'fsdp', 'tp'), may hold values from -6 to 6
- ln_gain: bfloat16 [2048], P(('fsdp', 'tp')), may hold values from 0.099609375 to 1.8984375
- ln_bias: bfloat16 [2048], P(('fsdp', 'tp')), may hold values from -3 to 3
- qkv_weight: bfloat16 [2048, 3, 2048], P('fsdp', None, 'tp'), may hold values from -0.125 to 0.125
- qkv_bias: bfloat16 [3, 32, 64], P(None, 'tp', 'fsdp'), may hold values from -3 to 3
- out_weight: bfloat16 [2048, 2048], P('tp', 'fsdp'), may hold values from -1.5 to 1.5
- out_bias: bfloat16 [2048], P(('fsdp', 'tp')), may hold values from -3 to 3
- up_weight: bfloat16 [2048, 8192], P('fsdp', 'tp'), may hold values from -0.125 to 0.125
- up_bias: bfloat16 [128, 64], P('tp', 'fsdp'), may hold values from -3 to 3
- down_weight: bfloat16 [8192, 2048], P('tp', 'fsdp'), may hold values from -0.0625 to 0.0625
- down_bias: bfloat16 [2048], P(('fsdp', 'tp')), may hold values from -3 to 3
- cotangent: bfloat16 [2, 8, 1024, 2048], P(None, 'fsdp', 'tp'), may hold values from -40 to 40
Outputs:
- output: bfloat16 [2, 8, 1024, 2048], P(None, 'fsdp', 'tp')
- input_grad: bfloat16 [2, 8, 1024, 2048], P(None, 'fsdp', 'tp')
- ln_gain_grad: float32 [2048], P(('fsdp', 'tp'))
- ln_bias_grad: float32 [2048], P(('fsdp', 'tp'))
- qkv_weight_grad: float32 [2048, 3, 2048], P('fsdp', None, 'tp')
- qkv_bias_grad: float32 [3, 32, 64], P(None, 'tp', 'fsdp')
- out_weight_grad: float32 [2048, 2048], P('tp', 'fsdp')
- out_bias_grad: float32 [2048], P(('fsdp', 'tp'))
- up_weight_grad: float32 [2048, 8192], P('fsdp', 'tp')
- up_bias_grad: float32 [128, 64], P('tp', 'fsdp')
- down_weight_grad: float32 [8192, 2048], P('tp', 'fsdp')
- down_bias_grad: float32 [2048], P(('fsdp', 'tp'))
All inputs are finite; a program needn't handle non-finite values.
Results may differ from a plain program's by a relative error of at most 0.014.
Values may be sent and summed in bfloat16 or wider, within the bound.
No kernel may reach another device: no remote copies, remote signals or barrier semaphores. Data moves between devices by JAX's collectives and lax.ppermute only.
A program may use at most 320 MiB of HBM per device.

v0:
```python
import math
import jax
import jax.numpy as jnp
from jax import lax
from jax.sharding import PartitionSpec as P

ROT = 32
norm_epsilon = 1e-05
gelu_factor = 0.7978845608028654
mask_fill = -1e30


def layer_norm(resid_rows, gain_vec, shift_vec):
    row_mean = jnp.mean(resid_rows, axis=-1, keepdims=True)
    centred = resid_rows - row_mean
    row_var = jnp.mean(centred * centred, axis=-1, keepdims=True)
    return centred * lax.rsqrt(row_var + norm_epsilon) * gain_vec + shift_vec


def gelu_tanh(inner):
    return 0.5 * inner * (1.0 + jnp.tanh(gelu_factor * (inner + 0.044715 * inner * inner * inner)))


def rotary_tables(length, head_dim, rot_dim):
    half_rot = rot_dim // 2
    inv_freq = 10000.0 ** (-2.0 * jnp.arange(half_rot, dtype=jnp.float32) / rot_dim)
    angles = jnp.arange(length, dtype=jnp.float32)[:, None] * inv_freq[None, :]
    rest_ones = jnp.ones((length, head_dim - rot_dim), jnp.float32)
    cosine_table = jnp.concatenate([jnp.cos(angles), jnp.cos(angles), rest_ones], axis=1)
    sine_table = jnp.concatenate([jnp.sin(angles), jnp.sin(angles), 0.0 * rest_ones], axis=1)
    return (cosine_table, sine_table)


def rotate(head_vals, cosine_table, sine_table, rot_dim):
    half_rot = rot_dim // 2
    turned = jnp.concatenate(
        [
            -head_vals[..., half_rot:rot_dim],
            head_vals[..., :half_rot],
            0.0 * head_vals[..., rot_dim:],
        ],
        axis=-1,
    )
    return head_vals * cosine_table[:, None, :] + turned * sine_table[:, None, :]


def causal_mask(first_row, block_rows, key_count):
    row_ids = first_row + lax.broadcasted_iota(jnp.int32, (block_rows, key_count), 0)
    col_ids = lax.broadcasted_iota(jnp.int32, (block_rows, key_count), 1)
    return col_ids <= row_ids


def dot_rows(left, right):
    return lax.dot_general(
        left, right, (((0,), (0,)), ((), ())), preferred_element_type=jnp.float32
    )


def dot_cols(left, right):
    return lax.dot_general(
        left, right, (((1,), (1,)), ((), ())), preferred_element_type=jnp.float32
    )


def attend_forward(queries, keys_rot, values_low, score_scale):
    length = queries.shape[0]
    block_rows = min(512, length)
    out_blocks, lse_blocks = ([], [])
    for first_row in range(0, length, block_rows):
        last_row = first_row + block_rows
        scores = (
            jnp.einsum(
                "qhd,khd->hqk",
                queries[first_row:last_row],
                keys_rot[:last_row],
                preferred_element_type=jnp.float32,
            )
            * score_scale
        )
        scores = jnp.where(causal_mask(first_row, block_rows, last_row)[None], scores, mask_fill)
        row_max = jnp.max(scores, axis=-1, keepdims=True)
        exp_scores = jnp.exp(scores - row_max)
        denom_sum = jnp.sum(exp_scores, axis=-1, keepdims=True)
        prob_low = (exp_scores / denom_sum).astype(jnp.bfloat16)
        attn_block = jnp.einsum(
            "hqk,khd->qhd", prob_low, values_low[:last_row], preferred_element_type=jnp.float32
        )
        out_blocks.append(attn_block.astype(jnp.bfloat16))
        lse_blocks.append((row_max + jnp.log(denom_sum))[..., 0])
    return (jnp.concatenate(out_blocks, axis=0), jnp.concatenate(lse_blocks, axis=1))


def attend_backward(queries, keys_rot, values_low, lse_rows, attn_grad, score_scale):
    length = queries.shape[0]
    block_rows = min(512, length)
    key_grad = jnp.zeros(queries.shape, jnp.float32)
    value_grad = jnp.zeros(queries.shape, jnp.float32)
    query_blocks = []
    for first_row in range(0, length, block_rows):
        last_row = first_row + block_rows
        query_block = queries[first_row:last_row]
        grad_block = attn_grad[first_row:last_row]
        scores = (
            jnp.einsum(
                "qhd,khd->hqk", query_block, keys_rot[:last_row], preferred_element_type=jnp.float32
            )
            * score_scale
        )
        scores = jnp.where(causal_mask(first_row, block_rows, last_row)[None], scores, mask_fill)
        probs = jnp.exp(scores - lse_rows[:, first_row:last_row, None])
        prob_low = probs.astype(jnp.bfloat16)
        value_grad = value_grad.at[:last_row].add(
            jnp.einsum("hqk,qhd->khd", prob_low, grad_block, preferred_element_type=jnp.float32)
        )
        prob_grad = jnp.einsum(
            "qhd,khd->hqk", grad_block, values_low[:last_row], preferred_element_type=jnp.float32
        )
        inner_sum = jnp.sum(probs * prob_grad, axis=-1, keepdims=True)
        score_grad = (probs * (prob_grad - inner_sum)).astype(jnp.bfloat16)
        query_blocks.append(
            jnp.einsum(
                "hqk,khd->qhd", score_grad, keys_rot[:last_row], preferred_element_type=jnp.float32
            )
            * score_scale
        )
        key_grad = key_grad.at[:last_row].add(
            jnp.einsum("hqk,qhd->khd", score_grad, query_block, preferred_element_type=jnp.float32)
            * score_scale
        )
    return (jnp.concatenate(query_blocks, axis=0), key_grad, value_grad)


def shards(
    inputs,
    ln_gain,
    ln_bias,
    qkv_weight,
    qkv_bias,
    out_weight,
    out_bias,
    up_weight,
    up_bias,
    down_weight,
    down_bias,
    cotangent,
):
    micro_count = inputs.shape[0]
    seq_count = inputs.shape[1]
    model_width = inputs.shape[3]
    length = inputs.shape[2] * lax.axis_size("tp")
    local_heads = qkv_bias.shape[1]
    head_dim = qkv_bias.shape[2] * lax.axis_size("fsdp")
    score_scale = 1.0 / math.sqrt(head_dim)
    cosine_table, sine_table = rotary_tables(length, head_dim, ROT)
    gain_full, shift_full, bias_out_full, bias_down_full = (
        lax.all_gather(ln_gain, ("fsdp", "tp"), axis=0, tiled=True),
        lax.all_gather(ln_bias, ("fsdp", "tp"), axis=0, tiled=True),
        lax.all_gather(out_bias, ("fsdp", "tp"), axis=0, tiled=True),
        lax.all_gather(down_bias, ("fsdp", "tp"), axis=0, tiled=True),
    )
    gain_vec = gain_full.astype(jnp.float32)
    shift_vec = shift_full.astype(jnp.float32)
    bias_both = bias_out_full.astype(jnp.float32) + bias_down_full.astype(jnp.float32)
    gain_total = jnp.zeros((model_width,), jnp.float32)
    shift_total = jnp.zeros((model_width,), jnp.float32)
    bias_total = jnp.zeros((model_width,), jnp.float32)
    grad_totals = None
    outputs, input_grads = ([], [])

    def rot_back(head_grads):
        pull_back = jax.vjp(
            lambda head_vals: rotate(head_vals, cosine_table, sine_table, ROT),
            jnp.zeros_like(head_grads),
        )[1]
        return pull_back(head_grads)[0]

    for batch_index in range(micro_count):
        w_qkv, b_qkv, w_out, w_up, b_up, w_down = (
            lax.all_gather(qkv_weight, "fsdp", axis=0, tiled=True),
            lax.all_gather(qkv_bias, "fsdp", axis=2, tiled=True),
            lax.all_gather(out_weight, "fsdp", axis=1, tiled=True),
            lax.all_gather(up_weight, "fsdp", axis=0, tiled=True),
            lax.all_gather(up_bias, "fsdp", axis=1, tiled=True),
            lax.all_gather(down_weight, "fsdp", axis=1, tiled=True),
        )
        w_qkv_flat = w_qkv.reshape(model_width, -1)
        resid_rows = inputs[batch_index].astype(jnp.float32)
        normed_low = layer_norm(resid_rows, gain_vec, shift_vec).astype(jnp.bfloat16)
        normed_full = lax.all_gather(normed_low, "tp", axis=1, tiled=True)
        flat_normed = normed_full.reshape(-1, model_width)
        qkv_proj = jnp.dot(
            flat_normed, w_qkv_flat, preferred_element_type=jnp.float32
        ) + b_qkv.reshape(-1).astype(jnp.float32)
        qkv_proj = qkv_proj.reshape(seq_count, length, 3, local_heads, head_dim)
        queries = rotate(qkv_proj[:, :, 0], cosine_table, sine_table, ROT).astype(jnp.bfloat16)
        keys_rot = rotate(qkv_proj[:, :, 1], cosine_table, sine_table, ROT).astype(jnp.bfloat16)
        values_low = qkv_proj[:, :, 2].astype(jnp.bfloat16)
        attn_low, lse_rows = lax.map(
            lambda seq_args: attend_forward(seq_args[0], seq_args[1], seq_args[2], score_scale),
            (queries, keys_rot, values_low),
        )
        attn_flat = attn_low.reshape(-1, local_heads * head_dim)
        pre_act = jnp.dot(flat_normed, w_up, preferred_element_type=jnp.float32) + b_up.reshape(
            -1
        ).astype(jnp.float32)
        act_low = gelu_tanh(pre_act).astype(jnp.bfloat16)
        branch_terms = jnp.dot(attn_flat, w_out, preferred_element_type=jnp.float32) + jnp.dot(
            act_low, w_down, preferred_element_type=jnp.float32
        )
        branch_local = lax.psum_scatter(
            branch_terms.reshape(seq_count, length, model_width).astype(jnp.bfloat16),
            "tp",
            scatter_dimension=1,
            tiled=True,
        ).astype(jnp.float32)
        outputs.append((resid_rows + branch_local + bias_both).astype(jnp.bfloat16))
        w_qkv, w_out, w_up, w_down = (
            lax.all_gather(qkv_weight, "fsdp", axis=0, tiled=True),
            lax.all_gather(out_weight, "fsdp", axis=1, tiled=True),
            lax.all_gather(up_weight, "fsdp", axis=0, tiled=True),
            lax.all_gather(down_weight, "fsdp", axis=1, tiled=True),
        )
        w_qkv_flat = w_qkv.reshape(model_width, -1)
        cot_local = cotangent[batch_index]
        cot_full = lax.all_gather(cot_local, "tp", axis=1, tiled=True)
        cot_flat = cot_full.reshape(-1, model_width)
        bias_total = bias_total + jnp.sum(cot_local.astype(jnp.float32), axis=(0, 1))
        out_w_grad = dot_rows(attn_flat, cot_flat)
        down_w_grad = dot_rows(act_low, cot_flat)
        attn_grad = dot_cols(cot_flat, w_out).astype(jnp.bfloat16)
        act_grad = dot_cols(cot_flat, w_down)
        pre_grad = jax.vjp(gelu_tanh, pre_act)[1](act_grad)[0].astype(jnp.bfloat16)
        up_w_grad = dot_rows(flat_normed, pre_grad)
        up_b_grad = jnp.sum(pre_grad.astype(jnp.float32), axis=0).reshape(b_up.shape)
        attn_grad_heads = attn_grad.reshape(seq_count, length, local_heads, head_dim)
        query_grad, key_grad, value_grad = lax.map(
            lambda seq_args: attend_backward(
                seq_args[0], seq_args[1], seq_args[2], seq_args[3], seq_args[4], score_scale
            ),
            (queries, keys_rot, values_low, lse_rows, attn_grad_heads),
        )
        qkv_grad = jnp.stack([rot_back(query_grad), rot_back(key_grad), value_grad], axis=2).astype(
            jnp.bfloat16
        )
        qkv_grad = qkv_grad.reshape(-1, 3 * local_heads * head_dim)
        qkv_w_grad = dot_rows(flat_normed, qkv_grad).reshape(w_qkv.shape)
        qkv_b_grad = jnp.sum(qkv_grad.astype(jnp.float32), axis=0).reshape(3, local_heads, head_dim)
        normed_grad = dot_cols(qkv_grad, w_qkv_flat) + dot_cols(pre_grad, w_up)
        normed_local = lax.psum_scatter(
            normed_grad.reshape(seq_count, length, model_width).astype(jnp.bfloat16),
            "tp",
            scatter_dimension=1,
            tiled=True,
        ).astype(jnp.float32)
        norm_back = jax.vjp(layer_norm, resid_rows, gain_vec, shift_vec)[1]
        rows_grad, gain_grad, shift_grad = norm_back(normed_local)
        input_grads.append((cot_local.astype(jnp.float32) + rows_grad).astype(jnp.bfloat16))
        gain_total = gain_total + gain_grad
        shift_total = shift_total + shift_grad
        big_grads = (qkv_w_grad, qkv_b_grad, out_w_grad, up_w_grad, up_b_grad, down_w_grad)
        big_grads = (
            lax.psum_scatter(
                big_grads[0].astype(jnp.bfloat16), "fsdp", scatter_dimension=0, tiled=True
            ).astype(jnp.float32),
            lax.psum_scatter(
                big_grads[1].astype(jnp.bfloat16), "fsdp", scatter_dimension=2, tiled=True
            ).astype(jnp.float32),
            lax.psum_scatter(
                big_grads[2].astype(jnp.bfloat16), "fsdp", scatter_dimension=1, tiled=True
            ).astype(jnp.float32),
            lax.psum_scatter(
                big_grads[3].astype(jnp.bfloat16), "fsdp", scatter_dimension=0, tiled=True
            ).astype(jnp.float32),
            lax.psum_scatter(
                big_grads[4].astype(jnp.bfloat16), "fsdp", scatter_dimension=1, tiled=True
            ).astype(jnp.float32),
            lax.psum_scatter(
                big_grads[5].astype(jnp.bfloat16), "fsdp", scatter_dimension=1, tiled=True
            ).astype(jnp.float32),
        )
        if grad_totals is None:
            grad_totals = big_grads
        else:
            grad_totals = tuple((earlier + later for earlier, later in zip(grad_totals, big_grads)))
    gain_sum, shift_sum, bias_sum = (
        lax.psum_scatter(gain_total, ("fsdp", "tp"), scatter_dimension=0, tiled=True),
        lax.psum_scatter(shift_total, ("fsdp", "tp"), scatter_dimension=0, tiled=True),
        lax.psum_scatter(bias_total, ("fsdp", "tp"), scatter_dimension=0, tiled=True),
    )
    return (
        jnp.stack(outputs, axis=0),
        jnp.stack(input_grads, axis=0),
        gain_sum,
        shift_sum,
        grad_totals[0],
        grad_totals[1],
        grad_totals[2],
        bias_sum,
        grad_totals[3],
        grad_totals[4],
        grad_totals[5],
        bias_sum,
    )


def solution(mesh):
    return jax.shard_map(
        shards,
        mesh=mesh,
        in_specs=(
            P(None, "fsdp", "tp", None),
            P(("fsdp", "tp")),
            P(("fsdp", "tp")),
            P("fsdp", None, "tp"),
            P(None, "tp", "fsdp"),
            P("tp", "fsdp"),
            P(("fsdp", "tp")),
            P("fsdp", "tp"),
            P("tp", "fsdp"),
            P("tp", "fsdp"),
            P(("fsdp", "tp")),
            P(None, "fsdp", "tp", None),
        ),
        out_specs=(
            P(None, "fsdp", "tp", None),
            P(None, "fsdp", "tp", None),
            P(("fsdp", "tp")),
            P(("fsdp", "tp")),
            P("fsdp", None, "tp"),
            P(None, "tp", "fsdp"),
            P("tp", "fsdp"),
            P(("fsdp", "tp")),
            P("fsdp", "tp"),
            P("tp", "fsdp"),
            P("tp", "fsdp"),
            P(("fsdp", "tp")),
        ),
        check_vma=False,
    )
```

profile of v0, /device:TPU:0, one launch (start us, length us, event | category | flops | bytes accessed | tf_op | source)
XLA Modules:
  0.0 1753.6 jit_solution(16200274292250818931)
XLA Ops:
  8.0 3.1 fusion.196
  13.0 42.9 %all-reduce.28 = (bf16[2048]{0:T(1024)(128)(2,1)S(1)}, bf16[2048]{0:T(1024)(128)(2,1)S(1)}, bf16[2048]{0:T(1024)(128)(2,1)}, bf16[2048]{0:T(1024)(128)(2,1)}) all-reduce(bf16[2048]{0:T(1024)(128)(2,1)S(1)} %dynamic-update-slice.25, bf16[2048]{0:T(1024)(128)(2,1)S(1)} %dynamic-update-slice.24, ...), channel_id=1, replica_groups=mesh['fsdp'=8,'tp'=4] {'fsdp','tp'}, use_global_device_ids=true, to_apply=%add.17 | all-reduce | flops 8192 | bytes 32768
  64.3 26.0 %all_gather.63 = bf16[32,64]{0,1:T(8,128)(2,1)S(1)} all-gather(bf16[32,8]{0,1:T(8,128)(2,1)S(1)} %copy-done.84), channel_id=1, replica_groups=mesh['fsdp'=8,'tp'=4] {'fsdp'}, dimensions={1}, use_global_device_ids=true | all-gather | bytes 4608 | tf_op jit(solution)/shard_map/all_gather | solution.py:183
  91.0 30.5 %all_gather.60 = bf16[3,8,64]{1,0,2:T(4,128)(2,1)S(1)} all-gather(bf16[3,8,8]{1,0,2:T(4,128)(2,1)S(1)} %copy.106), channel_id=1, replica_groups=mesh['fsdp'=8,'tp'=4] {'fsdp'}, dimensions={2}, use_global_device_ids=true | all-gather | bytes 3456 | tf_op jit(solution)/shard_map/all_gather | solution.py:180
  124.1 5.4 fusion.133
  130.6 5.8 all-gather.23.cloned.1.call-done
  136.4 4.6 fusion.130
  142.0 30.9 %all-gather.21.cloned.1.call-done = bf16[1,1024,2048]{2,1,0:T(8,128)(2,1)} async-done(((bf16[1,256,2048]{2,1,0:T(8,128)(2,1)}), bf16[1,1024,2048]{2,1,0:T(8,128)(2,1)}) %all-gather.21.cloned.1.call-update) | async-done | bytes 4194320 | tf_op jit(solution)/shard_map/all_gather | solution.py:189
  172.9 102.4 %all-gather.13.cloned.1.call-done = bf16[2048,3,512]{0,2,1:T(8,128)(2,1)} async-done(((bf16[256,3,512]{0,2,1:T(8,128)(2,1)}), bf16[2048,3,512]{0,2,1:T(8,128)(2,1)}) %all-gather.13.cloned.1.call-update) | async-done | bytes 6291472 | tf_op jit(solution)/shard_map/all_gather | solution.py:179
  275.3 11.9 convolution_add_fusion
  287.2 6.7 copy.111
  304.3 5.7 all-gather.11.cloned.1.call-done
  310.0 11.7 convolution_add_fusion.1
  321.7 6.7 copy.108
  342.7 3.2 fusion.202
  345.9 3.8 fusion
  351.7 5.7 fusion.154
  382.6 3.2 fusion.203
  385.8 3.7 fusion.1
  391.6 12.1 multiply_reduce_fusion.1
  404.8 12.1 multiply_convert_fusion.1
  419.6 12.3 multiply_reduce_fusion
  431.9 12.0 multiply_convert_fusion
  443.9 4.2 fusion.146
  464.4 3.7 fusion.64
  468.0 5.7 fusion.157
  473.7 9.0 fusion.155
  492.0 6.2 fusion.136
  500.7 3.7 fusion.67
  504.4 9.0 fusion.120
  513.3 8.6 fusion.116
  522.2 6.2 add_bitcast_fusion.1
  531.3 14.4 fusion.53
  545.7 17.0 all-gather.19.cloned.1.call-done
  562.8 20.6 %fusion.205 = (bf16[2048]{0:T(1024)(128)(2,1)}, bf16[1024,2048]{1,0:T(8,128)(2,1)S(1)}) fusion(bf16[2048,2048]{1,0:T(8,128)(2,1)} %all-gather.19.cloned.1.call-done, bf16[1,1,1024,2048]{3,2,1,0:T(8,128)(2,1)} %all-gather.25.cloned.1.call-done, f32[1024,2048]{1,0:T(8,128)} %fusion.53, f32[2048]{0:T(1024)S(1)} %copy-done.78), kind=kOutput, calls=%fused_computation.335 | convolution fusion | flops 8644458496 | bytes 25178112 | tf_op jit(solution)/shard_map/dot_general | solution.py:60
  583.4 11.3 fusion.208
  594.7 12.6 fusion.35
  607.3 15.1 fusion.57
  622.5 20.8 %fusion.206 = (bf16[2048]{0:T(1024)(128)(2,1)}, bf16[1024,2048]{1,0:T(8,128)(2,1)}) fusion(bf16[2048,2048]{1,0:T(8,128)(2,1)} %all-gather.19.cloned.1.call-done, bf16[1,1,1024,2048]{3,2,1,0:T(8,128)(2,1)S(1)} %copy-done.87, f32[1024,2048]{1,0:T(8,128)} %fusion.57, f32[2048]{0:T(1024)S(1)} %copy-done.78), kind=kOutput, calls=%fused_computation.336 | convolution fusion | flops 8644458496 | bytes 25178112 | tf_op jit(solution)/shard_map/dot_general | solution.py:60
  643.3 12.9 fusion.207
  656.2 12.6 fusion.34
  668.8 15.5 fusion.190
  684.3 4.5 fusion.32
  688.9 15.7 fusion.191
  704.5 4.4 fusion.33
  709.0 12.2 convolution_convert_fusion.4
  721.3 11.7 convolution_convert_fusion.5
  733.0 14.1 convolution_convert_fusion.3
  747.2 14.6 convolution_convert_fusion.2
  761.9 16.2 convolution_convert_fusion
  778.2 16.2 convolution_convert_fusion.1
  798.5 34.4 %all-reduce.29 = (bf16[3,8,64]{2,1,0:T(8,128)(2,1)S(1)}, bf16[3,8,64]{2,1,0:T(8,128)(2,1)S(1)}, bf16[32,64]{1,0:T(8,128)(2,1)S(1)}, bf16[32,64]{1,0:T(8,128)(2,1)S(1)}) all-reduce(bf16[3,8,64]{2,1,0:T(8,128)(2,1)S(1)} %copy-done.69, bf16[3,8,64]{2,1,0:T(8,128)(2,1)S(1)} %copy-done.68, ...), channel_id=13, replica_groups=mesh['fsdp'=8,'tp'=4] {'fsdp'}, use_global_device_ids=true, to_apply=%region_35.36.clone | all-reduce | flops 7168 | bytes 28672
  839.0 4.8 reduce-scatter.17.cloned.1.call-done
  843.8 47.1 %reduce-scatter.19.cloned.1.call-done = bf16[1,256,2048]{2,1,0:T(8,128)(2,1)} async-done(((bf16[1,1024,2048]{2,1,0:T(8,128)(2,1)}), bf16[1,256,2048]{2,1,0:T(8,128)(2,1)}) %reduce-scatter.19.cloned.1.call-update) | async-done | bytes 1048592 | tf_op jit(solution)/shard_map/reduce_scatter | solution.py:210
  890.9 4.8 fusion.106
  895.7 43.0 %all-reduce.27 = (f32[2048]{0:T(1024)S(1)}, f32[2048]{0:T(1024)S(1)}, f32[2048]{0:T(1024)S(1)}) all-reduce(f32[2048]{0:T(1024)S(1)} %add.457, f32[2048]{0:T(1024)S(1)} %add.458, f32[2048]{0:T(1024)S(1)} %add.462), channel_id=8, replica_groups=mesh['fsdp'=8,'tp'=4] {'fsdp','tp'}, use_global_device_ids=true, to_apply=%region_26.27.clone | all-reduce | flops 6144 | bytes 49152
  940.0 3.3 fusion.159
  947.1 66.8 %reduce-scatter.27.cloned.1.call-done = bf16[256,3,512]{2,0,1:T(8,128)(2,1)} async-done(((bf16[2048,3,512]{2,0,1:T(8,128)(2,1)}), bf16[256,3,512]{2,0,1:T(8,128)(2,1)}) %reduce-scatter.27.cloned.1.call-update) | async-done | bytes 786448 | tf_op jit(solution)/shard_map/reduce_scatter | solution.py:262
  1013.8 121.0 %reduce-scatter.25.cloned.1.call-done = bf16[256,3,512]{2,0,1:T(8,128)(2,1)} async-done(((bf16[2048,3,512]{2,0,1:T(8,128)(2,1)}), bf16[256,3,512]{2,0,1:T(8,128)(2,1)}) %reduce-scatter.25.cloned.1.call-update) | async-done | bytes 786448 | tf_op jit(solution)/shard_map/reduce_scatter | solution.py:262
  1137.6 148.9 %reduce-scatter.33.cloned.1.call-done = bf16[256,2048]{1,0:T(8,128)(2,1)} async-done(((bf16[2048,2048]{1,0:T(8,128)(2,1)}), bf16[256,2048]{1,0:T(8,128)(2,1)}) %reduce-scatter.33.cloned.1.call-update) | async-done | bytes 1048592 | tf_op jit(solution)/shard_map/reduce_scatter | solution.py:271
  1286.5 152.0 %reduce-scatter.35.cloned.1.call-done = bf16[256,2048]{1,0:T(8,128)(2,1)} async-done(((bf16[2048,2048]{1,0:T(8,128)(2,1)}), bf16[256,2048]{1,0:T(8,128)(2,1)}) %reduce-scatter.35.cloned.1.call-update) | async-done | bytes 1048592 | tf_op jit(solution)/shard_map/reduce_scatter | solution.py:271
  1438.5 3.2 convert_add_fusion.1
  1441.7 148.8 %reduce-scatter.39.cloned.1.call-done = bf16[2048,256]{1,0:T(8,128)(2,1)} async-done(((bf16[2048,2048]{1,0:T(8,128)(2,1)}), bf16[2048,256]{1,0:T(8,128)(2,1)}) %reduce-scatter.39.cloned.1.call-update) | async-done | bytes 1048592 | tf_op jit(solution)/shard_map/reduce_scatter | solution.py:277
  1590.6 152.4 %reduce-scatter.37.cloned.1.call-done = bf16[2048,256]{1,0:T(8,128)(2,1)} async-done(((bf16[2048,2048]{1,0:T(8,128)(2,1)}), bf16[2048,256]{1,0:T(8,128)(2,1)}) %reduce-scatter.37.cloned.1.call-update) | async-done | bytes 1048592 | tf_op jit(solution)/shard_map/reduce_scatter | solution.py:277
  (374 shorter events, 125.9 us)
Async XLA Ops:
  7.2 48.7 %copy-start.4 = (bf16[2,1,256,2048]{3,2,1,0:T(8,128)(2,1)S(1)}, bf16[2,1,256,2048]{3,2,1,0:T(8,128)(2,1)}, u32[]{:S(2)}) copy-start(bf16[2,1,256,2048]{3,2,1,0:T(8,128)(2,1)} %param.36) | copy-start | bytes 6291460
  7.2 116.9 %all-gather.15.cloned.1.call-start = ((), (), s32[]{:S(2)}) async-start(), calls=%async_computation.14 | async-start | bytes 2359296 | tf_op jit(solution)/shard_map/all_gather | solution.py:181
  8.0 116.2 %all-gather.25.cloned.1.call-start = ((), (), s32[]{:S(2)}) async-start(), calls=%async_computation.31 | async-start | bytes 5242880 | tf_op jit(solution)/shard_map/all_gather | solution.py:225
  11.1 125.2 %all-gather.23.cloned.1.call-start = ((), (), s32[]{:S(2)}) async-start(), calls=%async_computation.30 | async-start | bytes 5242880 | tf_op jit(solution)/shard_map/all_gather | solution.py:225
  11.9 161.0 %all-gather.21.cloned.1.call-start = ((), (), s32[]{:S(2)}) async-start(), calls=%async_computation.18 | async-start | bytes 5242880 | tf_op jit(solution)/shard_map/all_gather | solution.py:189
  59.8 215.5 %all-gather.13.cloned.1.call-start = ((), (), s32[]{:S(2)}) async-start(), calls=%async_computation.13 | async-start | bytes 7077888 | tf_op jit(solution)/shard_map/all_gather | solution.py:179
  61.1 249.0 %all-gather.11.cloned.1.call-start = ((), (), s32[]{:S(2)}) async-start(), calls=%async_computation.12 | async-start | bytes 5242880 | tf_op jit(solution)/shard_map/all_gather | solution.py:189
  61.6 469.7 %all-gather.17.cloned.1.call-start = ((), (), s32[]{:S(2)}) async-start(), calls=%async_computation.15 | async-start | bytes 9437184 | tf_op jit(solution)/shard_map/all_gather | solution.py:182
  62.4 500.4 %all-gather.19.cloned.1.call-start = ((), (), s32[]{:S(2)}) async-start(), calls=%async_computation.16 | async-start | bytes 9437184 | tf_op jit(solution)/shard_map/all_gather | solution.py:184
  63.1 771.1 %reduce-scatter.29.cloned.1.call-start = ((), (), s32[]{:S(2)}) async-start(), calls=%async_computation.24 | async-start | bytes 2359296 | tf_op jit(solution)/shard_map/reduce_scatter | solution.py:268
  122.9 217.3 %copy-start.25 = (f32[1024,64]{0,1:T(8,128)}, f32[1024,64]{0,1:T(8,128)S(1)}, u32[]{:S(2)}) copy-start(f32[1024,64]{0,1:T(8,128)S(1)} %maximum_maximum_fusion.1) | copy-start | bytes 786436
  124.1 12.3 copy-start.89
  345.9 5.8 copy-start
  351.7 5.8 slice-start.4
  351.7 5.8 slice-start.5
  385.8 5.8 copy-start.1
  385.8 5.8 copy-start.31
  391.6 12.1 copy-start.60
  404.8 12.1 copy-start.21
  419.6 28.4 %copy-start.14 = (f32[1,512,8,64]{1,3,2,0:T(8,128)}, f32[1,512,8,64]{1,3,2,0:T(8,128)S(1)}, u32[]{:S(2)}) copy-start(f32[1,512,8,64]{1,3,2,0:T(8,128)S(1)} %fusion.147) | copy-start | bytes 3145732
  473.7 9.5 copy-start.61
  482.7 9.3 copy-start.38
  482.7 351.5 %reduce-scatter.31.cloned.1.call-start = ((), (), s32[]{:S(2)}) async-start(), calls=%async_computation.25 | async-start | bytes 2359296 | tf_op jit(solution)/shard_map/reduce_scatter | solution.py:268
  483.2 15.0 slice-start
  484.5 16.1 copy-start.57
  492.0 6.2 slice-start.1
  492.0 6.2 copy-start.36
  504.4 9.0 copy-start.30
  504.4 9.0 copy-start.41
  513.3 8.9 copy-start.15
  513.3 8.9 copy-start.29
  522.0 314.2 %reduce-scatter.23.cloned.1.call-start = ((), (), s32[]{:S(2)}) async-start(), calls=%async_computation.21 | async-start | bytes 5242880 | tf_op jit(solution)/shard_map/reduce_scatter | solution.py:249
  522.2 6.2 copy-start.39
  522.2 6.2 copy-start.40
  531.3 31.5 %copy-start.78 = (f32[2048]{0:T(1024)S(1)}, f32[2048]{0:T(1024)}, u32[]{:S(2)}) copy-start(f32[2048]{0:T(1024)} %reshape.1680) | copy-start | bytes 24580
  562.7 20.6 %copy-start.85 = (bf16[2048,2048]{1,0:T(8,128)(2,1)S(1)}, bf16[2048,2048]{1,0:T(8,128)(2,1)}, u32[]{:S(2)}) copy-start(bf16[2048,2048]{1,0:T(8,128)(2,1)} %all-gather.17.cloned.1.call-done) | copy-start | bytes 25165828
  583.4 11.3 copy-start.98
  583.4 11.3 copy-start.46
  607.3 228.9 %reduce-scatter.21.cloned.1.call-start = ((), (), s32[]{:S(2)}) async-start(), calls=%async_computation.20 | async-start | bytes 5242880 | tf_op jit(solution)/shard_map/reduce_scatter | solution.py:249
  607.3 15.1 copy-start.87
  607.3 35.9 %slice-start.6 = ((s8[8388608]{0:T(1024)(128)(4,1)}), s8[4194304]{0:T(1024)(128)(4,1)S(1)}, s32[]{:S(2)}) async-start(s8[8388608]{0:T(1024)(128)(4,1)} %bitcast.456), calls=%async_computation.38 | async-start | bytes 8388608
  622.5 20.8 %slice-start.7 = ((s8[8388608]{0:T(1024)(128)(4,1)}), s8[4194304]{0:T(1024)(128)(4,1)S(1)}, s32[]{:S(2)}) async-start(s8[8388608]{0:T(1024)(128)(4,1)} %bitcast.456), calls=%async_computation.39 | async-start | bytes 8388608
  668.7 175.1 %reduce-scatter.17.cloned.1.call-start = ((), (), s32[]{:S(2)}) async-start(), calls=%async_computation.17 | async-start | bytes 5242880 | tf_op jit(solution)/shard_map/reduce_scatter | solution.py:210
  668.8 15.5 copy-start.56
  668.8 15.5 copy-start.90
  688.8 202.1 %reduce-scatter.19.cloned.1.call-start = ((), (), s32[]{:S(2)}) async-start(), calls=%async_computation.19 | async-start | bytes 5242880 | tf_op jit(solution)/shard_map/reduce_scatter | solution.py:210
  688.8 15.7 copy-start.58
  688.9 15.7 copy-start.91
  708.9 304.9 %reduce-scatter.27.cloned.1.call-start = ((), (), s32[]{:S(2)}) async-start(), calls=%async_computation.23 | async-start | bytes 7077888 | tf_op jit(solution)/shard_map/reduce_scatter | solution.py:262
  721.2 413.6 %reduce-scatter.25.cloned.1.call-start = ((), (), s32[]{:S(2)}) async-start(), calls=%async_computation.22 | async-start | bytes 7077888 | tf_op jit(solution)/shard_map/reduce_scatter | solution.py:262
  733.0 553.5 %reduce-scatter.33.cloned.1.call-start = ((), (), s32[]{:S(2)}) async-start(), calls=%async_computation.26 | async-start | bytes 9437184 | tf_op jit(solution)/shard_map/reduce_scatter | solution.py:271
  747.2 691.3 %reduce-scatter.35.cloned.1.call-start = ((), (), s32[]{:S(2)}) async-start(), calls=%async_computation.27 | async-start | bytes 9437184 | tf_op jit(solution)/shard_map/reduce_scatter | solution.py:271
  761.9 828.7 %reduce-scatter.39.cloned.1.call-start = ((), (), s32[]{:S(2)}) async-start(), calls=%async_computation.29 | async-start | bytes 9437184 | tf_op jit(solution)/shard_map/reduce_scatter | solution.py:277
  778.1 964.8 %reduce-scatter.37.cloned.1.call-start = ((), (), s32[]{:S(2)}) async-start(), calls=%async_computation.28 | async-start | bytes 9437184 | tf_op jit(solution)/shard_map/reduce_scatter | solution.py:277
  794.5 41.7 %copy-start.5 = (bf16[2,1,256,2048]{3,2,1,0:T(8,128)(2,1)S(1)}, bf16[2,1,256,2048]{3,2,1,0:T(8,128)(2,1)}, u32[]{:S(2)}) copy-start(bf16[2,1,256,2048]{3,2,1,0:T(8,128)(2,1)} %param.36) | copy-start | bytes 6291460
  794.5 41.7 %copy-start.63 = (f32[2048]{0:T(1024)S(1)}, f32[2048]{0:T(1024)}, u32[]{:S(2)}) copy-start(f32[2048]{0:T(1024)} %copy-done.62) | copy-start | bytes 24580
  794.5 41.7 %copy-start.65 = (f32[256]{0:T(256)S(1)}, f32[256]{0:T(256)}, u32[]{:S(2)}) copy-start(f32[256]{0:T(256)} %copy-done.64) | copy-start | bytes 3076
  794.5 41.7 %copy-start.67 = (f32[256]{0:T(256)S(1)}, f32[256]{0:T(256)}, u32[]{:S(2)}) copy-start(f32[256]{0:T(256)} %copy-done.66) | copy-start | bytes 3076
  794.5 44.4 %copy-start.77 = (f32[256]{0:T(256)S(1)}, f32[256]{0:T(256)}, u32[]{:S(2)}) copy-start(f32[256]{0:T(256)} %copy-done.76) | copy-start | bytes 3076
  794.5 44.4 %copy-start.75 = (f32[256]{0:T(256)S(1)}, f32[256]{0:T(256)}, u32[]{:S(2)}) copy-start(f32[256]{0:T(256)} %copy-done.74) | copy-start | bytes 3076
  794.5 96.4 %copy-start.71 = (f32[256]{0:T(256)S(1)}, f32[256]{0:T(256)}, u32[]{:S(2)}) copy-start(f32[256]{0:T(256)} %copy-done.70) | copy-start | bytes 3076
  794.6 96.4 %copy-start.73 = (f32[256]{0:T(256)S(1)}, f32[256]{0:T(256)}, u32[]{:S(2)}) copy-start(f32[256]{0:T(256)} %copy-done.72) | copy-start | bytes 3076
  836.1 54.8 %copy-start.13 = (bf16[1,256,2048]{2,1,0:T(8,128)(2,1)S(1)}, bf16[1,256,2048]{2,1,0:T(8,128)(2,1)}, u32[]{:S(2)}) copy-start(bf16[1,256,2048]{2,1,0:T(8,128)(2,1)} %reduce-scatter.23.cloned.1.call-done) | copy-start | bytes 3145732
  939.4 806.7 %copy-start.97 = (f32[64]{0:T(128)}, f32[64]{0:T(128)S(1)}, u32[]{:S(2)}) copy-start(f32[64]{0:T(128)S(1)} %dynamic-slice.70) | copy-start | bytes 772
  (63 other events, 201.3 us)
Sparse Core Ops, SparseCore 0:
  10.1 54.6 all-gather.14
  67.0 32.7 all-gather.24
  101.8 34.4 all-gather.22
  138.4 34.4 all-gather.20
  175.3 99.9 all-gather.12
  277.3 32.6 all-gather.10
  312.1 124.9 all-gather.16
  439.1 123.5 all-gather.18
  566.3 66.2 reduce-scatter.28
  636.5 67.0 reduce-scatter.30
  706.1 43.5 reduce-scatter.22
  752.2 44.4 reduce-scatter.20
  799.3 44.5 reduce-scatter.16
  846.4 44.4 reduce-scatter.18
  894.4 119.4 reduce-scatter.26
  1017.3 117.5 reduce-scatter.24
  1138.3 148.1 reduce-scatter.32
  1290.4 147.9 reduce-scatter.34
  1442.1 148.4 reduce-scatter.38
  1594.5 148.4 reduce-scatter.36
where the time goes:
time: 1760 us; the launch traced here: 1750 us
  waiting for transfers between devices  1010 us (57%)
  matrix products  388 us (22%)
  blocking collectives  177 us (10%)
  other arithmetic  111 us (6%)
  local copies, waits for them, and re-layouts  52.3 us (3%)
    reduce_scatter x2, waiting for transfers between devices, shards(): lax.psum_scatter(big_grads[5].astype(jnp.bfloat16), 'fsdp', scatter_dimen...  301 us
    reduce_scatter x2, waiting for transfers between devices, shards(): lax.psum_scatter(big_grads[3].astype(jnp.bfloat16), 'fsdp', scatter_dimen...  301 us
    reduce_scatter x2, waiting for transfers between devices, shards(): lax.psum_scatter(big_grads[0].astype(jnp.bfloat16), 'fsdp', scatter_dimen...  188 us
    unnamed x3, blocking collectives  120 us
    all_gather x1, waiting for transfers between devices, shards(): lax.all_gather(qkv_weight, 'fsdp', axis=0, tiled=True)  102 us
    dot_general x8, matrix products, dot_cols(): lax.dot_general(left, right, (((1,), (1,)), ((), ())), preferred_element_...  101 us
    dot_general x8, matrix products, dot_rows(): lax.dot_general(left, right, (((0,), (0,)), ((), ())), preferred_element_...  92.4 us
    reduce_scatter x2, waiting for transfers between devices, shards(): lax.psum_scatter(branch_terms.reshape(seq_count, length, model_width).ast...  51.9 us
  transfers between devices with their start and end apart: 20, of which 13 were waited for; matrix products, arithmetic and copies ran while one was open for 30% of the time, Pallas kernels for 0%

commit v1 on v0

--- a/solution.py
+++ b/solution.py
@@ -8,6 +8,23 @@
 norm_epsilon = 1e-05
 gelu_factor = 0.7978845608028654
 mask_fill = -1e30
+
+
+def laid_out(blocks, dim):
+    shape = list(blocks.shape[1:])
+    shape[dim] *= blocks.shape[0]
+    return jnp.moveaxis(blocks, 0, dim).reshape(shape)
+
+
+def collect(shard, axis, dim):
+    size = lax.axis_size(axis)
+    right = [(i, (i + 1) % size) for i in range(size)]
+    blocks = [shard]
+    while len(blocks) < size:
+        blocks.append(lax.ppermute(blocks[-1], axis, right))
+    here = lax.axis_index(axis)
+    blocks = jnp.stack(blocks)[(here - jnp.arange(size)) % size]
+    return laid_out(blocks, dim)
 
 
 def layer_norm(resid_rows, gain_vec, shift_vec):
@@ -186,7 +203,7 @@
         w_qkv_flat = w_qkv.reshape(model_width, -1)
         resid_rows = inputs[batch_index].astype(jnp.float32)
         normed_low = layer_norm(resid_rows, gain_vec, shift_vec).astype(jnp.bfloat16)
-        normed_full = lax.all_gather(normed_low, "tp", axis=1, tiled=True)
+        normed_full = collect(normed_low, "tp", 1)
         flat_normed = normed_full.reshape(-1, model_width)
         qkv_proj = jnp.dot(
             flat_normed, w_qkv_flat, preferred_element_type=jnp.float32

time: 1760 us -> 1710 us (0.972)
  waiting for transfers between devices: 1010 us -> 923 us
    all_gather x1, waiting for transfers between devices: 102 us -> 15.7 us  [shards(): lax.all_gather(qkv_weight, 'fsdp', axis=0, tiled=True)]
    ppermute x0 -> x6, waiting for transfers between devices: none -> 76.7 us  [collect(): blocks.append(lax.ppermute(blocks[-1], axis, right))]
    all_gather x2 -> x0, waiting for transfers between devices: 36.6 us -> none  [shards(): normed_full = lax.all_gather(normed_low, 'tp', axis=1, tiled=True)]
  transfers between devices with their start and end apart: 20 -> 24, of which waited for: 13 -> 12; matrix products, arithmetic and copies ran while one was open for 30% -> 32% of each run, Pallas kernels for 0% -> 0%
where the time goes in v1:
time: 1710 us; the launch traced here: 1700 us
  waiting for transfers between devices  923 us (54%)
  matrix products  387 us (23%)
  blocking collectives  179 us (10%)
  other arithmetic  119 us (7%)
  local copies, waits for them, and re-layouts  62.2 us (4%)
    reduce_scatter x2, waiting for transfers between devices, shards(): lax.psum_scatter(big_grads[5].astype(jnp.bfloat16), 'fsdp', scatter_dimen...  301 us
    reduce_scatter x2, waiting for transfers between devices, shards(): lax.psum_scatter(big_grads[3].astype(jnp.bfloat16), 'fsdp', scatter_dimen...  301 us
    reduce_scatter x2, waiting for transfers between devices, shards(): lax.psum_scatter(big_grads[0].astype(jnp.bfloat16), 'fsdp', scatter_dimen...  188 us
    unnamed x3, blocking collectives  122 us
    dot_general x8, matrix products, dot_cols(): lax.dot_general(left, right, (((1,), (1,)), ((), ())), preferred_element_...  101 us
    dot_general x8, matrix products, dot_rows(): lax.dot_general(left, right, (((0,), (0,)), ((), ())), preferred_element_...  92.2 us
    ppermute x6, waiting for transfers between devices, collect(): blocks.append(lax.ppermute(blocks[-1], axis, right))  76.7 us
    reduce_scatter x2, waiting for transfers between devices, shards(): lax.psum_scatter(branch_terms.reshape(seq_count, length, model_width).ast...  38.8 us
  transfers between devices with their start and end apart: 24, of which 12 were waited for; matrix products, arithmetic and copies ran while one was open for 32% of the time, Pallas kernels for 0%

profile of v1, /device:TPU:0, one launch (start us, length us, event | category | flops | bytes accessed | tf_op | source)
XLA Modules:
  0.0 1703.0 jit_solution(5527172170580617320)
XLA Ops:
  14.9 44.3 %all-reduce.28 = (bf16[2048]{0:T(1024)(128)(2,1)S(1)}, bf16[2048]{0:T(1024)(128)(2,1)S(1)}, bf16[2048]{0:T(1024)(128)(2,1)}, bf16[2048]{0:T(1024)(128)(2,1)}) all-reduce(bf16[2048]{0:T(1024)(128)(2,1)S(1)} %dynamic-update-slice.25, bf16[2048]{0:T(1024)(128)(2,1)S(1)} %dynamic-update-slice.24, ...), channel_id=1, replica_groups=mesh['fsdp'=8,'tp'=4] {'fsdp','tp'}, use_global_device_ids=true, to_apply=%add.17 | all-reduce | flops 8192 | bytes 32768
  64.8 13.5 collective-permute-done
  78.3 5.4 collective-permute-start.1
  83.9 26.0 %collective-permute-done.3 = bf16[1,256,2048]{2,1,0:T(8,128)(2,1)} collective-permute-done((bf16[1,256,2048]{2,1,0:T(8,128)(2,1)S(1)}, bf16[1,256,2048]{2,1,0:T(8,128)(2,1)}, u32[]{:S(2)}, u32[]{:S(2)}) %collective-permute-start.3) | collective-permute-done | bytes 1048608 | tf_op jit(solution)/shard_map/ppermute | solution.py:24
  111.0 10.2 collective-permute-done.1
  123.9 27.0 %collective-permute-done.4 = bf16[1,256,2048]{2,1,0:T(8,128)(2,1)} collective-permute-done((bf16[1,256,2048]{2,1,0:T(8,128)(2,1)}, bf16[1,256,2048]{2,1,0:T(8,128)(2,1)}, u32[]{:S(2)}, u32[]{:S(2)}) %collective-permute-start.4) | collective-permute-done | bytes 1048608 | tf_op jit(solution)/shard_map/ppermute | solution.py:24
  150.9 4.4 collective-permute-start.5
  155.4 26.3 %all_gather.56 = bf16[32,64]{0,1:T(8,128)(2,1)S(1)} all-gather(bf16[32,8]{0,1:T(8,128)(2,1)S(1)} %copy-done.86), channel_id=1, replica_groups=mesh['fsdp'=8,'tp'=4] {'fsdp'}, dimensions={1}, use_global_device_ids=true | all-gather | bytes 4608 | tf_op jit(solution)/shard_map/all_gather | solution.py:200
  182.4 31.0 %all_gather.53 = bf16[3,8,64]{1,0,2:T(4,128)(2,1)S(1)} all-gather(bf16[3,8,8]{1,0,2:T(4,128)(2,1)S(1)} %copy.106), channel_id=1, replica_groups=mesh['fsdp'=8,'tp'=4] {'fsdp'}, dimensions={2}, use_global_device_ids=true | all-gather | bytes 3456 | tf_op jit(solution)/shard_map/all_gather | solution.py:197
  216.1 3.6 maximum_bitcast_fusion
  219.8 5.1 gather_fusion
  224.9 3.6 maximum_bitcast_fusion.1
  228.6 5.0 gather_fusion.1
  233.6 5.4 fusion.131
  240.0 4.6 fusion.128
  245.6 15.7 all-gather.9.cloned.1.call-done
  261.3 11.7 convolution_add_fusion
  273.1 6.7 copy.111
  290.2 10.7 convolution_add_fusion.1
  300.9 6.5 copy.108
  325.2 3.8 fusion
  331.1 6.1 fusion.152
  365.4 3.7 fusion.1
  371.2 11.9 multiply_reduce_fusion.1
  384.2 12.4 multiply_convert_fusion.1
  399.3 12.4 multiply_reduce_fusion
  411.6 12.1 multiply_convert_fusion
  423.8 4.0 fusion.144
  444.2 3.7 fusion.54
  447.9 5.7 fusion.155
  453.6 9.0 fusion.153
  472.0 5.9 fusion.134
  480.3 3.7 fusion.57
  484.0 8.9 fusion.118
  493.0 8.5 fusion.114
  501.8 6.2 add_bitcast_fusion.1
  510.8 14.5 fusion.208
  525.4 20.7 %fusion.205 = (bf16[2048]{0:T(1024)(128)(2,1)}, bf16[1024,2048]{1,0:T(8,128)(2,1)S(1)}) fusion(bf16[2048,2048]{1,0:T(8,128)(2,1)} %all-gather.15.cloned.1.call-done, bf16[1,1,1024,2048]{3,2,1,0:T(8,128)(2,1)} %all-gather.19.cloned.1.call-done, f32[1024,2048]{1,0:T(8,128)} %fusion.208, f32[2048]{0:T(1024)S(1)} %copy-done.80), kind=kOutput, calls=%fused_computation.346 | convolution fusion | flops 8644458496 | bytes 25178112 | tf_op jit(solution)/shard_map/dot_general | solution.py:77
  546.1 11.4 fusion.210
  557.4 12.5 fusion.35
  570.1 15.2 fusion.207
  585.2 20.7 %fusion.206 = (bf16[2048]{0:T(1024)(128)(2,1)}, bf16[1024,2048]{1,0:T(8,128)(2,1)}) fusion(bf16[2048,2048]{1,0:T(8,128)(2,1)} %all-gather.15.cloned.1.call-done, bf16[1,1,1024,2048]{3,2,1,0:T(8,128)(2,1)S(1)} %copy-done.89, f32[1024,2048]{1,0:T(8,128)} %fusion.207, f32[2048]{0:T(1024)S(1)} %copy-done.80), kind=kOutput, calls=%fused_computation.347 | convolution fusion | flops 8644458496 | bytes 25178112 | tf_op jit(solution)/shard_map/dot_general | solution.py:77
  606.0 13.0 fusion.209
  618.9 12.4 fusion.34
  631.4 15.4 fusion.190
  646.9 4.4 fusion.32
  651.4 15.7 fusion.191
  667.1 4.4 fusion.33
  671.5 12.2 convolution_convert_fusion.4
  683.8 11.5 convolution_convert_fusion.5
  695.4 14.1 convolution_convert_fusion.3
  709.5 15.0 convolution_convert_fusion.2
  724.6 16.0 convolution_convert_fusion
  740.6 16.1 convolution_convert_fusion.1
  761.0 34.4 %all-reduce.29 = (bf16[3,8,64]{2,1,0:T(8,128)(2,1)S(1)}, bf16[3,8,64]{2,1,0:T(8,128)(2,1)S(1)}, bf16[32,64]{1,0:T(8,128)(2,1)S(1)}, bf16[32,64]{1,0:T(8,128)(2,1)S(1)}) all-reduce(bf16[3,8,64]{2,1,0:T(8,128)(2,1)S(1)} %copy-done.75, bf16[3,8,64]{2,1,0:T(8,128)(2,1)S(1)} %copy-done.74, ...), channel_id=13, replica_groups=mesh['fsdp'=8,'tp'=4] {'fsdp'}, use_global_device_ids=true, to_apply=%region_35.36.clone | all-reduce | flops 7168 | bytes 28672
  801.6 38.8 %reduce-scatter.19.cloned.1.call-done = bf16[1,256,2048]{2,1,0:T(8,128)(2,1)} async-done(((bf16[1,1024,2048]{2,1,0:T(8,128)(2,1)}), bf16[1,256,2048]{2,1,0:T(8,128)(2,1)}) %reduce-scatter.19.cloned.1.call-update) | async-done | bytes 1048592 | tf_op jit(solution)/shard_map/reduce_scatter | solution.py:227
  840.4 4.8 fusion.104
  845.2 43.0 %all-reduce.27 = (f32[2048]{0:T(1024)S(1)}, f32[2048]{0:T(1024)S(1)}, f32[2048]{0:T(1024)S(1)}) all-reduce(f32[2048]{0:T(1024)S(1)} %add.496, f32[2048]{0:T(1024)S(1)} %add.497, f32[2048]{0:T(1024)S(1)} %add.501), channel_id=8, replica_groups=mesh['fsdp'=8,'tp'=4] {'fsdp','tp'}, use_global_device_ids=true, to_apply=%region_26.27.clone | all-reduce | flops 6144 | bytes 49152
  896.6 66.8 %reduce-scatter.27.cloned.1.call-done = bf16[256,3,512]{2,0,1:T(8,128)(2,1)} async-done(((bf16[2048,3,512]{2,0,1:T(8,128)(2,1)}), bf16[256,3,512]{2,0,1:T(8,128)(2,1)}) %reduce-scatter.27.cloned.1.call-update) | async-done | bytes 786448 | tf_op jit(solution)/shard_map/reduce_scatter | solution.py:279
  963.5 121.0 %reduce-scatter.25.cloned.1.call-done = bf16[256,3,512]{2,0,1:T(8,128)(2,1)} async-done(((bf16[2048,3,512]{2,0,1:T(8,128)(2,1)}), bf16[256,3,512]{2,0,1:T(8,128)(2,1)}) %reduce-scatter.25.cloned.1.call-update) | async-done | bytes 786448 | tf_op jit(solution)/shard_map/reduce_scatter | solution.py:279
  1087.2 148.9 %reduce-scatter.33.cloned.1.call-done = bf16[256,2048]{1,0:T(8,128)(2,1)} async-done(((bf16[2048,2048]{1,0:T(8,128)(2,1)}), bf16[256,2048]{1,0:T(8,128)(2,1)}) %reduce-scatter.33.cloned.1.call-update) | async-done | bytes 1048592 | tf_op jit(solution)/shard_map/reduce_scatter | solution.py:288
  1236.1 152.0 %reduce-scatter.35.cloned.1.call-done = bf16[256,2048]{1,0:T(8,128)(2,1)} async-done(((bf16[2048,2048]{1,0:T(8,128)(2,1)}), bf16[256,2048]{1,0:T(8,128)(2,1)}) %reduce-scatter.35.cloned.1.call-update) | async-done | bytes 1048592 | tf_op jit(solution)/shard_map/reduce_scatter | solution.py:288
  1391.3 148.7 %reduce-scatter.39.cloned.1.call-done = bf16[2048,256]{1,0:T(8,128)(2,1)} async-done(((bf16[2048,2048]{1,0:T(8,128)(2,1)}), bf16[2048,256]{1,0:T(8,128)(2,1)}) %reduce-scatter.39.cloned.1.call-update) | async-done | bytes 1048592 | tf_op jit(solution)/shard_map/reduce_scatter | solution.py:294
  1540.0 152.3 %reduce-scatter.37.cloned.1.call-done = bf16[2048,256]{1,0:T(8,128)(2,1)} async-done(((bf16[2048,2048]{1,0:T(8,128)(2,1)}), bf16[2048,256]{1,0:T(8,128)(2,1)}) %reduce-scatter.37.cloned.1.call-update) | async-done | bytes 1048592 | tf_op jit(solution)/shard_map/reduce_scatter | solution.py:294
  (391 shorter events, 145.5 us)
Async XLA Ops:
  7.2 226.4 %all-gather.11.cloned.1.call-start = ((), (), s32[]{:S(2)}) async-start(), calls=%async_computation.13 | async-start | bytes 2359296 | tf_op jit(solution)/shard_map/all_gather | solution.py:198
  8.0 51.3 %copy-start.4 = (bf16[2,1,256,2048]{3,2,1,0:T(8,128)(2,1)S(1)}, bf16[2,1,256,2048]{3,2,1,0:T(8,128)(2,1)}, u32[]{:S(2)}) copy-start(bf16[2,1,256,2048]{3,2,1,0:T(8,128)(2,1)} %param.36) | copy-start | bytes 6291460
  8.0 225.6 %all-gather.19.cloned.1.call-start = ((), (), s32[]{:S(2)}) async-start(), calls=%async_computation.29 | async-start | bytes 5242880 | tf_op jit(solution)/shard_map/all_gather | solution.py:242
  11.3 228.7 %all-gather.17.cloned.1.call-start = ((), (), s32[]{:S(2)}) async-start(), calls=%async_computation.28 | async-start | bytes 5242880 | tf_op jit(solution)/shard_map/all_gather | solution.py:242
  12.0 249.3 %all-gather.9.cloned.1.call-start = ((), (), s32[]{:S(2)}) async-start(), calls=%async_computation.12 | async-start | bytes 7077888 | tf_op jit(solution)/shard_map/all_gather | solution.py:196
  13.3 497.6 %all-gather.13.cloned.1.call-start = ((), (), s32[]{:S(2)}) async-start(), calls=%async_computation.14 | async-start | bytes 9437184 | tf_op jit(solution)/shard_map/all_gather | solution.py:199
  13.9 511.5 %all-gather.15.cloned.1.call-start = ((), (), s32[]{:S(2)}) async-start(), calls=%async_computation.15 | async-start | bytes 9437184 | tf_op jit(solution)/shard_map/all_gather | solution.py:201
  59.2 155.1 %copy-start.64 = (f32[2048]{0:T(1024)}, f32[2048]{0:T(1024)S(1)}, u32[]{:S(2)}) copy-start(f32[2048]{0:T(1024)S(1)} %convert_element_type.508) | copy-start | bytes 24580
  59.6 154.8 %copy-start.66 = (f32[256]{0:T(256)}, f32[256]{0:T(256)S(1)}, u32[]{:S(2)}) copy-start(f32[256]{0:T(256)S(1)} %broadcast_multiply_fusion.1) | copy-start | bytes 3076
  59.6 154.7 %copy-start.68 = (f32[256]{0:T(256)}, f32[256]{0:T(256)S(1)}, u32[]{:S(2)}) copy-start(f32[256]{0:T(256)S(1)} %broadcast_multiply_fusion) | copy-start | bytes 3076
  59.6 95.7 %copy-start.81 = (bf16[3,8,8]{2,1,0:T(8,128)(2,1)S(1)}, bf16[3,8,8]{2,1,0:T(8,128)(2,1)}, u32[]{:S(2)}) copy-start(bf16[3,8,8]{2,1,0:T(8,128)(2,1)} %param.40) | copy-start | bytes 1156
  59.7 95.8 %copy-start.86 = (bf16[32,8]{0,1:T(8,128)(2,1)S(1)}, bf16[32,8]{0,1:T(8,128)(2,1)}, u32[]{:S(2)}) copy-start(bf16[32,8]{0,1:T(8,128)(2,1)} %param.44) | copy-start | bytes 1540
  60.4 155.7 %copy-start.70 = (f32[256]{0:T(256)}, f32[256]{0:T(256)S(1)}, u32[]{:S(2)}) copy-start(f32[256]{0:T(256)S(1)} %fusion.180) | copy-start | bytes 3076
  61.0 155.2 %copy-start.72 = (f32[256]{0:T(256)}, f32[256]{0:T(256)S(1)}, u32[]{:S(2)}) copy-start(f32[256]{0:T(256)S(1)} %fusion.181) | copy-start | bytes 3076
  61.8 16.5 collective-permute-start
  62.2 47.7 %collective-permute-start.3 = (bf16[1,256,2048]{2,1,0:T(8,128)(2,1)S(1)}, bf16[1,256,2048]{2,1,0:T(8,128)(2,1)}, u32[]{:S(2)}, u32[]{:S(2)}) collective-permute-start(bf16[1,256,2048]{2,1,0:T(8,128)(2,1)S(1)} %get-tuple-element.370), channel_id=1, source_target_pairs={{0,1},{1,2},{2,3},{3,0},{4,5},{5,6},{6,7},{7,4},{8,9},{9,10},{10,1... | collective-permute-start | bytes 3145736 | tf_op jit(solution)/shard_map/ppermute | solution.py:24
  78.3 42.8 %collective-permute-start.1 = (bf16[1,256,2048]{2,1,0:T(8,128)(2,1)}, bf16[1,256,2048]{2,1,0:T(8,128)(2,1)}, u32[]{:S(2)}, u32[]{:S(2)}) collective-permute-start(bf16[1,256,2048]{2,1,0:T(8,128)(2,1)} %collective-permute-done), channel_id=1, source_target_pairs={{0,1},{1,2},{2,3},{3,0},{4,5},{5,6},{6,7},{7,4},{8,9},{9,10},{10,1... | collective-permute-start | bytes 3145736 | tf_op jit(solution)/shard_map/ppermute | solution.py:24
  83.8 713.0 %reduce-scatter.29.cloned.1.call-start = ((), (), s32[]{:S(2)}) async-start(), calls=%async_computation.22 | async-start | bytes 2359296 | tf_op jit(solution)/shard_map/reduce_scatter | solution.py:285
  109.9 41.0 %collective-permute-start.4 = (bf16[1,256,2048]{2,1,0:T(8,128)(2,1)}, bf16[1,256,2048]{2,1,0:T(8,128)(2,1)}, u32[]{:S(2)}, u32[]{:S(2)}) collective-permute-start(bf16[1,256,2048]{2,1,0:T(8,128)(2,1)} %collective-permute-done.3), channel_id=1, source_target_pairs={{0,1},{1,2},{2,3},{3,0},{4,5},{5,6},{6,7},{7,4},{8,9},{9,10},{10,1... | collective-permute-start | bytes 3145736 | tf_op jit(solution)/shard_map/ppermute | solution.py:24
  110.8 108.9 %copy-start.27 = (f32[1024,64]{0,1:T(8,128)}, f32[1024,64]{0,1:T(8,128)S(1)}, u32[]{:S(2)}) copy-start(f32[1024,64]{0,1:T(8,128)S(1)} %maximum_maximum_fusion) | copy-start | bytes 786436
  110.9 208.8 %copy-start.25 = (f32[1024,64]{0,1:T(8,128)}, f32[1024,64]{0,1:T(8,128)S(1)}, u32[]{:S(2)}) copy-start(f32[1024,64]{0,1:T(8,128)S(1)} %maximum_maximum_fusion.1) | copy-start | bytes 786436
  121.1 95.0 %collective-permute-start.2 = (bf16[1,256,2048]{2,1,0:T(8,128)(2,1)}, bf16[1,256,2048]{2,1,0:T(8,128)(2,1)}, u32[]{:S(2)}, u32[]{:S(2)}) collective-permute-start(bf16[1,256,2048]{2,1,0:T(8,128)(2,1)} %collective-permute-done.1), channel_id=1, source_target_pairs={{0,1},{1,2},{2,3},{3,0},{4,5},{5,6},{6,7},{7,4},{8,9},{9,10},{10,1... | collective-permute-start | bytes 3145736 | tf_op jit(solution)/shard_map/ppermute | solution.py:24
  150.9 74.1 %collective-permute-start.5 = (bf16[1,256,2048]{2,1,0:T(8,128)(2,1)}, bf16[1,256,2048]{2,1,0:T(8,128)(2,1)}, u32[]{:S(2)}, u32[]{:S(2)}) collective-permute-start(bf16[1,256,2048]{2,1,0:T(8,128)(2,1)} %collective-permute-done.4), channel_id=1, source_target_pairs={{0,1},{1,2},{2,3},{3,0},{4,5},{5,6},{6,7},{7,4},{8,9},{9,10},{10,1... | collective-permute-start | bytes 3145736 | tf_op jit(solution)/shard_map/ppermute | solution.py:24
  371.1 11.9 copy-start.62
  384.2 12.4 copy-start.21
  399.3 28.6 %copy-start.14 = (f32[1,512,8,64]{1,3,2,0:T(8,128)}, f32[1,512,8,64]{1,3,2,0:T(8,128)S(1)}, u32[]{:S(2)}) copy-start(f32[1,512,8,64]{1,3,2,0:T(8,128)S(1)} %fusion.145) | copy-start | bytes 3145732
  453.6 9.5 copy-start.63
  462.7 9.3 copy-start.38
  462.7 334.1 %reduce-scatter.31.cloned.1.call-start = ((), (), s32[]{:S(2)}) async-start(), calls=%async_computation.23 | async-start | bytes 2359296 | tf_op jit(solution)/shard_map/reduce_scatter | solution.py:285
  463.2 14.7 slice-start
  464.5 15.8 copy-start.59
  484.0 9.0 copy-start.30
  484.0 9.0 copy-start.41
  501.5 297.2 %reduce-scatter.23.cloned.1.call-start = ((), (), s32[]{:S(2)}) async-start(), calls=%async_computation.19 | async-start | bytes 5242880 | tf_op jit(solution)/shard_map/reduce_scatter | solution.py:266
  510.8 14.5 copy-start.80
  525.4 20.7 %copy-start.87 = (bf16[2048,2048]{1,0:T(8,128)(2,1)S(1)}, bf16[2048,2048]{1,0:T(8,128)(2,1)}, u32[]{:S(2)}) copy-start(bf16[2048,2048]{1,0:T(8,128)(2,1)} %all-gather.13.cloned.1.call-done) | copy-start | bytes 25165828
  546.1 11.4 copy-start.100
  546.1 11.4 copy-start.48
  570.0 228.7 %reduce-scatter.21.cloned.1.call-start = ((), (), s32[]{:S(2)}) async-start(), calls=%async_computation.18 | async-start | bytes 5242880 | tf_op jit(solution)/shard_map/reduce_scatter | solution.py:266
  570.0 15.2 copy-start.89
  570.0 35.9 %slice-start.6 = ((s8[8388608]{0:T(1024)(128)(4,1)}), s8[4194304]{0:T(1024)(128)(4,1)S(1)}, s32[]{:S(2)}) async-start(s8[8388608]{0:T(1024)(128)(4,1)} %bitcast.468), calls=%async_computation.36 | async-start | bytes 8388608
  585.2 20.7 %slice-start.7 = ((s8[8388608]{0:T(1024)(128)(4,1)}), s8[4194304]{0:T(1024)(128)(4,1)S(1)}, s32[]{:S(2)}) async-start(s8[8388608]{0:T(1024)(128)(4,1)} %bitcast.468), calls=%async_computation.37 | async-start | bytes 8388608
  631.4 170.2 %reduce-scatter.17.cloned.1.call-start = ((), (), s32[]{:S(2)}) async-start(), calls=%async_computation.16 | async-start | bytes 5242880 | tf_op jit(solution)/shard_map/reduce_scatter | solution.py:227
  631.4 15.5 copy-start.58
  631.4 15.5 copy-start.92
  651.3 189.1 %reduce-scatter.19.cloned.1.call-start = ((), (), s32[]{:S(2)}) async-start(), calls=%async_computation.17 | async-start | bytes 5242880 | tf_op jit(solution)/shard_map/reduce_scatter | solution.py:227
  651.3 15.7 copy-start.60
  651.3 15.7 copy-start.93
  671.5 292.0 %reduce-scatter.27.cloned.1.call-start = ((), (), s32[]{:S(2)}) async-start(), calls=%async_computation.21 | async-start | bytes 7077888 | tf_op jit(solution)/shard_map/reduce_scatter | solution.py:279
  683.7 400.7 %reduce-scatter.25.cloned.1.call-start = ((), (), s32[]{:S(2)}) async-start(), calls=%async_computation.20 | async-start | bytes 7077888 | tf_op jit(solution)/shard_map/reduce_scatter | solution.py:279
  695.3 540.8 %reduce-scatter.33.cloned.1.call-start = ((), (), s32[]{:S(2)}) async-start(), calls=%async_computation.24 | async-start | bytes 9437184 | tf_op jit(solution)/shard_map/reduce_scatter | solution.py:288
  709.4 678.6 %reduce-scatter.35.cloned.1.call-start = ((), (), s32[]{:S(2)}) async-start(), calls=%async_computation.25 | async-start | bytes 9437184 | tf_op jit(solution)/shard_map/reduce_scatter | solution.py:288
  724.5 815.5 %reduce-scatter.39.cloned.1.call-start = ((), (), s32[]{:S(2)}) async-start(), calls=%async_computation.27 | async-start | bytes 9437184 | tf_op jit(solution)/shard_map/reduce_scatter | solution.py:294
  740.5 951.8 %reduce-scatter.37.cloned.1.call-start = ((), (), s32[]{:S(2)}) async-start(), calls=%async_computation.26 | async-start | bytes 9437184 | tf_op jit(solution)/shard_map/reduce_scatter | solution.py:294
  756.8 41.9 %copy-start.5 = (bf16[2,1,256,2048]{3,2,1,0:T(8,128)(2,1)S(1)}, bf16[2,1,256,2048]{3,2,1,0:T(8,128)(2,1)}, u32[]{:S(2)}) copy-start(bf16[2,1,256,2048]{3,2,1,0:T(8,128)(2,1)} %param.36) | copy-start | bytes 6291460
  756.8 41.9 %copy-start.65 = (f32[2048]{0:T(1024)S(1)}, f32[2048]{0:T(1024)}, u32[]{:S(2)}) copy-start(f32[2048]{0:T(1024)} %copy-done.64) | copy-start | bytes 24580
  756.8 41.9 %copy-start.67 = (f32[256]{0:T(256)S(1)}, f32[256]{0:T(256)}, u32[]{:S(2)}) copy-start(f32[256]{0:T(256)} %copy-done.66) | copy-start | bytes 3076
  756.8 41.9 %copy-start.69 = (f32[256]{0:T(256)S(1)}, f32[256]{0:T(256)}, u32[]{:S(2)}) copy-start(f32[256]{0:T(256)} %copy-done.68) | copy-start | bytes 3076
  756.9 44.7 %copy-start.79 = (f32[256]{0:T(256)S(1)}, f32[256]{0:T(256)}, u32[]{:S(2)}) copy-start(f32[256]{0:T(256)} %copy-done.78) | copy-start | bytes 3076
  756.9 44.7 %copy-start.77 = (f32[256]{0:T(256)S(1)}, f32[256]{0:T(256)}, u32[]{:S(2)}) copy-start(f32[256]{0:T(256)} %copy-done.76) | copy-start | bytes 3076
  756.9 83.5 %copy-start.71 = (f32[256]{0:T(256)S(1)}, f32[256]{0:T(256)}, u32[]{:S(2)}) copy-start(f32[256]{0:T(256)} %copy-done.70) | copy-start | bytes 3076
  756.9 83.5 %copy-start.73 = (f32[256]{0:T(256)S(1)}, f32[256]{0:T(256)}, u32[]{:S(2)}) copy-start(f32[256]{0:T(256)} %copy-done.72) | copy-start | bytes 3076
  798.7 41.7 %copy-start.13 = (bf16[1,256,2048]{2,1,0:T(8,128)(2,1)S(1)}, bf16[1,256,2048]{2,1,0:T(8,128)(2,1)}, u32[]{:S(2)}) copy-start(bf16[1,256,2048]{2,1,0:T(8,128)(2,1)} %reduce-scatter.23.cloned.1.call-done) | copy-start | bytes 3145732
  888.9 806.5 %copy-start.99 = (f32[64]{0:T(128)}, f32[64]{0:T(128)S(1)}, u32[]{:S(2)}) copy-start(f32[64]{0:T(128)S(1)} %dynamic-slice.70) | copy-start | bytes 772
  (69 other events, 272.2 us)
Sparse Core Ops, SparseCore 0:
  10.1 53.9 all-gather.10
  66.2 44.0 all-gather.18
  112.5 45.8 all-gather.16
  160.8 100.4 all-gather.8
  263.3 123.1 all-gather.12
  388.4 123.5 all-gather.14
  515.5 66.3 reduce-scatter.28
  586.0 67.0 reduce-scatter.30
  655.7 43.4 reduce-scatter.22
  701.7 44.4 reduce-scatter.20
  748.8 44.5 reduce-scatter.16
  795.9 44.4 reduce-scatter.18
  844.0 119.3 reduce-scatter.26
  966.9 117.4 reduce-scatter.24
  1087.9 148.1 reduce-scatter.32
  1240.0 147.9 reduce-scatter.34
  1391.6 148.4 reduce-scatter.38
  1544.0 148.3 reduce-scatter.36
